TPU v7x, 32 devices: a whole 2x2x4 slice. The times are simulated.
32 devices in a mesh: row: 4 (over y, x), col: 8 (over z, core).
Axes of the slice: x: 2, y: 2, z: 4, core: 2. Of those that a mesh axis runs over, the one named last changes fastest.
Arguments:
- features: bfloat16 [8192, 128], P(('row', 'col')), may hold values from -6 to 6
- weight: bfloat16 [128, 256], replicated, may hold values from -0.5 to 0.5
- cotangent: bfloat16 [8192, 256], P(('row', 'col')), may hold values from -6 to 6
- tile_values: bfloat16 [4, 8, 96, 128, 128], P('row', 'col'), may hold values from -0.3125 to 0.3125
- tile_rows: int32 [4, 8, 96], P('row', 'col'), may hold values from 0 to 15
- tile_cols: int32 [4, 8, 96], P('row', 'col'), may hold values from 0 to 7
- tile_counts: int32 [4, 8], P('row', 'col'), may hold values from 12 to 96, as said below
Outputs:
- output: bfloat16 [8192, 256], P(('row', 'col'))
- grad_features: bfloat16 [8192, 128], P(('row', 'col'))
- grad_weight: float32 [128, 256], replicated
Inputs may be any that keep to these rules, and one draw needn't show every extreme that they name: Slots 0 to tile_counts - 1 of a grid cell are live and the rest are ignored; the (row tile, column tile) pairs of a cell's live slots are distinct; some cells hold 96 live slots.
All inputs are finite; a program needn't handle non-finite values.
Results may differ from a plain program's by a relative error of at most 0.0049.
Values may be sent and summed in bfloat16 or wider, within the bound.
A program may use at most 128 MiB of HBM per device.

v0:
```python
import math

import jax
import jax.numpy as jnp
from jax import lax
from jax.sharding import PartitionSpec as P


def silu_slope(values):
    sigmoid_part = jax.nn.sigmoid(values)
    return sigmoid_part * (1.0 + values * (1.0 - sigmoid_part))


def tile_sums(slot_values, slot_rows, slot_cols, live_count, source, out_tiles, flipped):
    slot_total = slot_values.shape[0]
    tile_size = slot_values.shape[1]
    feature_width = source.shape[-1]
    group_size = math.gcd(slot_total, 32)
    block_turns = (live_count + group_size - 1) // group_size
    pattern = "gji,gjh->gih" if flipped else "gij,gjh->gih"
    wide_source = source.dtype == jnp.float32

    def add_group(step_index, running):
        first_slot = step_index * group_size
        group_values = lax.dynamic_slice_in_dim(slot_values, first_slot, group_size, 0)
        group_rows = lax.dynamic_slice_in_dim(slot_rows, first_slot, group_size, 0)
        group_cols = lax.dynamic_slice_in_dim(slot_cols, first_slot, group_size, 0)
        live_mask = first_slot + jnp.arange(group_size) < live_count
        group_values = jnp.where(
            live_mask[:, None, None], group_values, jnp.zeros((), group_values.dtype)
        )
        picked = jnp.take(source, group_cols, axis=0)
        products = jnp.einsum(pattern, group_values, picked, preferred_element_type=jnp.float32)
        return running.at[group_rows].add(products)

    empty = jnp.zeros((out_tiles, tile_size, feature_width), jnp.float32)
    return lax.fori_loop(0, block_turns, add_group, empty)


def local(features, weight, cotangent, tile_values, tile_rows, tile_cols, tile_counts):
    row_count = lax.axis_size("row")
    col_count = lax.axis_size("col")
    node_rows = features.shape[0]
    out_width = weight.shape[1]
    tile_size = tile_values.shape[-1]
    slot_values = tile_values[0, 0]
    slot_rows = tile_rows[0, 0]
    slot_cols = tile_cols[0, 0]
    live_count = tile_counts[0, 0]
    weight_wide = weight.astype(jnp.float32)
    row_tiles = col_count * node_rows // tile_size
    column_feats = lax.all_gather(features, "row", axis=0, tiled=True)
    source_tiles = column_feats.reshape(-1, tile_size, column_feats.shape[1])
    partial_value = tile_sums(
        slot_values, slot_rows, slot_cols, live_count, source_tiles, row_tiles, False
    )
    partial_value = partial_value.reshape(-1, partial_value.shape[-1])
    row_inputs = lax.psum(partial_value, "col")
    summed = jnp.dot(row_inputs, weight_wide, precision=lax.Precision.HIGHEST)
    own_rows = lax.dynamic_slice_in_dim(summed, lax.axis_index("col") * node_rows, node_rows, 0)
    full_cot = lax.all_gather(cotangent, "col", axis=0, tiled=True)
    grad_rows = (full_cot.astype(jnp.float32) * silu_slope(summed)).astype(jnp.bfloat16)
    output = jax.nn.silu(own_rows).astype(jnp.bfloat16)
    grad_tiles = grad_rows.reshape(-1, tile_size, out_width)
    col_tiles = row_count * node_rows // tile_size
    grad_cols = tile_sums(
        slot_values, slot_cols, slot_rows, live_count, grad_tiles, col_tiles, True
    ).reshape(-1, out_width)
    grad_mixed = lax.psum_scatter(grad_cols, "row", scatter_dimension=0, tiled=True)
    grad_in = jnp.dot(grad_mixed, weight_wide.T, precision=lax.Precision.HIGHEST)
    weight_term = jnp.dot(
        features.astype(jnp.float32).T, grad_mixed, precision=lax.Precision.HIGHEST
    )
    node_total = node_rows * row_count * col_count
    grad_weight = lax.psum(weight_term, ("row", "col")) * node_total ** (-0.5)
    return (output, grad_in.astype(jnp.bfloat16), grad_weight)


def solution(mesh):
    placed = (
        P(("row", "col"), None),
        P(),
        P(("row", "col"), None),
        P("row", "col", None, None, None),
        P("row", "col", None),
        P("row", "col", None),
        P("row", "col"),
    )
    return jax.shard_map(
        local,
        mesh=mesh,
        in_specs=placed,
        out_specs=(P(("row", "col"), None), P(("row", "col"), None), P()),
        check_vma=False,
    )
```

profile of v0, /device:TPU:0, one launch (start us, length us, event | category | flops | bytes accessed | tf_op | source)
XLA Modules:
  0.0 339.6 jit_solution(1586801475083655275)
XLA Ops:
  7.9 10.8 %all_gather.6 = bf16[1024,128]{1,0:T(8,128)(2,1)S(1)} all-gather(bf16[256,128]{1,0:T(8,128)(2,1)} %param.11), channel_id=1, replica_groups=mesh['row'=4,'col'=8] {'row'}, dimensions={0}, use_global_device_ids=true | all-gather | bytes 327680 | tf_op jit(solution)/shard_map/all_gather | solution.py:52
  18.6 0.1 broadcast_in_dim.58
  18.7 8.5 %while.20 = (s32[]{:T(128)}, f32[16,128,128]{2,1,0:T(8,128)S(1)}, s32[]{:T(128)}, s32[96]{0:T(128)}, s32[]{:T(128)}, /*index=5*/bf16[96,128,128]{2,1,0:T(8,128)(...) while((s32[]{:T(128)}, f32[16,128,128]{2,1,0:T(8,128)S(1)}, ...), condition=%wide.region_2.3_spmd, body=%wide.region_0.2_spmd.sunk | while | flops 135791968 | bytes 12588215 | solution.py:37
  18.8 0.7 compare_select_fusion.8
  19.5 1.4 compare_and_fusion.4
  20.9 1.6 gather_fusion
  22.5 2.0 fusion.36
  24.6 2.7 scatter_fusion
  27.3 1.0 copy-done.2
  28.3 0.0 all-gather.2.cloned.1.call-start
  28.3 0.7 all-gather.2.cloned.1.call-update
  29.0 0.0 reduce-scatter.2.cloned.1.call-start
  29.1 4.7 %copy.10 = bf16[1,1,96,128,128]{3,4,2,1,0:T(8,128)(2,1)} copy(bf16[1,1,96,128,128]{4,3,2,1,0:T(8,128)(2,1)} %bitcast.23) | data formatting | bytes 6291456 | tf_op args[3]
  33.8 71.3 %all-reduce.3.cloned.1.call-done = f32[2048,128]{1,0:T(8,128)} async-done(((f32[2048,128]{1,0:T(8,128)}), f32[2048,128]{1,0:T(8,128)}) %all-reduce.3.cloned.1.call-update) | async-done | bytes 1048592 | tf_op jit(solution)/shard_map/psum | solution.py:58
  105.0 22.9 %all-gather.2.cloned.1.call-done = bf16[2048,256]{1,0:T(8,128)(2,1)} async-done(((bf16[256,256]{1,0:T(8,128)(2,1)}), bf16[2048,256]{1,0:T(8,128)(2,1)}) %all-gather.2.cloned.1.call-update) | async-done | bytes 1048592 | tf_op jit(solution)/shard_map/all_gather | solution.py:61
  128.0 4.7 %multiply_convert_fusion = (bf16[2048,256]{1,0:T(8,128)(2,1)}, f32[2048,256]{1,0:T(8,128)}) fusion(bf16[2048,256]{1,0:T(8,128)(2,1)} %all-gather.2.cloned.1.call-done, f32[2048,128]{1,0:T(8,128)} %all-reduce.3.cloned.1.call-done, bf16[128,256]{1,0:T(8,128)(2,1)S(1)} %copy-done), kind=kOutput, calls=%fused_computation.36 | convolution fusion | flops 810549248 | bytes 5308416 | tf_op jit(solution)/shard_map/dot_general | solution.py:59
  132.7 0.1 broadcast_in_dim.59
  132.8 13.2 %while.21 = (s32[]{:T(128)}, f32[8,128,256]{2,1,0:T(8,128)S(1)}, s32[]{:T(128)}, s32[96]{0:T(128)S(1)}, s32[]{:T(128)}, /*index=5*/bf16[96,128,128]{1,2,0:T(8,12...) while((s32[]{:T(128)}, f32[8,128,256]{2,1,0:T(8,128)S(1)}, ...), condition=%wide.region_6.7_spmd, body=%wide.region_4.6_spmd.sunk | while | flops 271058272 | bytes 24122552 | solution.py:37
  132.8 0.1 compare_select_fusion.9
  132.9 0.7 compare_and_fusion.5
  133.6 1.9 gather_fusion.1
  135.5 3.9 %fusion.39 = f32[32,128,256]{2,1,0:T(8,128)} fusion(bf16[32,128,256]{2,1,0:T(8,128)(2,1)S(1)} %gather_fusion.1, pred[32]{0:T(512)(128)(4,1)S(1)} %get-tuple-element.252, bf16[96,128,128]{1,2,0:T(8,128)(2,1)} %get-tuple-element.319, s32[]{:T(128)S(6)} %select_n.80, pred[32]{0:T(512)(128)(4,1)S(1)} %get-tuple-element.253), kind=kOutput, calls=%fused_computation.20.clone.1 | convolution fusion | flops 270008320 | bytes 7340100 | tf_op jit(solution)/shard_map/while/body/gji,gjh->gih/dot_general | solution.py:33
  139.5 6.5 %scatter_fusion.1 = f32[8,128,256]{2,1,0:T(8,128)S(1)} fusion(f32[8,128,256]{2,1,0:T(8,128)S(1)} %get-tuple-element.303, s32[32]{0:T(128)S(1)} %compare_select_fusion.9, f32[32,128,256]{2,1,0:T(8,128)} %fusion.39), kind=kCustom, calls=%fused_computation.3.clone.1 | custom fusion | flops 1048576 | bytes 12583040 | tf_op jit(solution)/shard_map/while/body/scatter-add | solution.py:34
  146.0 1.0 copy-done.1
  146.9 0.0 all-reduce.5.cloned.1.call-start
  147.0 1.7 multiply_convert_fusion.1
  148.7 52.2 %reduce-scatter.2.cloned.1.call-done = f32[256,256]{1,0:T(8,128)} async-done(((f32[1024,256]{1,0:T(8,128)}), f32[256,256]{1,0:T(8,128)}) %reduce-scatter.2.cloned.1.call-update) | async-done | bytes 262160 | tf_op jit(solution)/shard_map/reduce_scatter | solution.py:69
  200.9 2.0 convolution_bitcast_fusion
  202.9 1.9 convolution_convert_fusion
  204.8 126.6 %all-reduce.5.cloned.1.call-done = f32[128,256]{0,1:T(8,128)} async-done(((f32[128,256]{0,1:T(8,128)}), f32[128,256]{0,1:T(8,128)}) %all-reduce.5.cloned.1.call-update) | async-done | bytes 131088 | tf_op jit(solution)/shard_map/psum | solution.py:75
  331.4 0.9 broadcast_multiply_fusion
  332.3 0.8 copy.12
  (16 shorter events, 0.1 us)
Async XLA Ops:
  7.2 120.8 %copy-start = (bf16[128,256]{1,0:T(8,128)(2,1)S(1)}, bf16[128,256]{1,0:T(8,128)(2,1)}, u32[]{:S(2)}) copy-start(bf16[128,256]{1,0:T(8,128)(2,1)} %param.12) | copy-start | bytes 196612
  7.2 97.8 %all-reduce.3.cloned.1.call-start = ((), (), s32[]{:S(2)}) async-start(), calls=%async_computation.1 | async-start | bytes 2097152 | tf_op jit(solution)/shard_map/psum | solution.py:58
  27.3 1.0 copy-start.2
  28.3 99.7 %all-gather.2.cloned.1.call-start = ((), (), s32[]{:S(2)}) async-start(), calls=%async_computation.2 | async-start | bytes 1179648 | tf_op jit(solution)/shard_map/all_gather | solution.py:61
  29.0 171.9 %reduce-scatter.2.cloned.1.call-start = ((), (), s32[]{:S(2)}) async-start(), calls=%async_computation.3 | async-start | bytes 1310720 | tf_op jit(solution)/shard_map/reduce_scatter | solution.py:69
  33.7 99.0 %copy-start.4 = (s32[96]{0:T(128)S(1)}, s32[96]{0:T(128)}, u32[]{:S(2)}) copy-start(s32[96]{0:T(128)} %get-tuple-element.341) | copy-start | bytes 1156
  33.7 99.0 %copy-start.5 = (s32[96]{0:T(128)S(1)}, s32[96]{0:T(128)}, u32[]{:S(2)}) copy-start(s32[96]{0:T(128)} %get-tuple-element.342) | copy-start | bytes 1156
  132.8 68.1 %copy-start.3 = (bf16[256,128]{1,0:T(8,128)(2,1)S(1)}, bf16[256,128]{1,0:T(8,128)(2,1)}, u32[]{:S(2)}) copy-start(bf16[256,128]{1,0:T(8,128)(2,1)} %param.11) | copy-start | bytes 196612
  145.9 1.0 copy-start.1
  146.9 184.5 %all-reduce.5.cloned.1.call-start = ((), (), s32[]{:S(2)}) async-start(), calls=%async_computation.4 | async-start | bytes 262144 | tf_op jit(solution)/shard_map/psum | solution.py:75
Sparse Core Ops, SparseCore 0:
  28.4 76.5 all-reduce.2
  106.6 21.3 all-gather.1
  147.1 53.7 reduce-scatter.1
  206.9 124.4 all-reduce.4
where the time goes:
time: 339 us; the launch traced here: 340 us
  waiting for transfers between devices  274 us (81%)
  other arithmetic  14.7 us (4%)
  matrix products  14.5 us (4%)
  between operations  14.5 us (4%)
  local copies, waits for them, and re-layouts  11.1 us (3%)
  blocking collectives  10.8 us (3%)
    psum x1, waiting for transfers between devices, local(): grad_weight = lax.psum(weight_term, ('row', 'col')) * node_total ** (-0.5)  127 us
    psum x1, waiting for transfers between devices, local(): row_inputs = lax.psum(partial_value, 'col')  71.3 us
    reduce_scatter x1, waiting for transfers between devices, local(): lax.psum_scatter(grad_cols, 'row', scatter_dimension=0, tiled=True)  52.2 us
    all_gather x1, waiting for transfers between devices, local(): full_cot = lax.all_gather(cotangent, 'col', axis=0, tiled=True)  22.9 us
    all_gather x1, blocking collectives, local(): column_feats = lax.all_gather(features, 'row', axis=0, tiled=True)  10.8 us
    scatter-add x2, other arithmetic, add_group(): return running.at[group_rows].add(products)  9.12 us
    unnamed x14, local copies, waits for them, and re-layouts  7.38 us
  transfers between devices with their start and end apart: 4, of which 4 were waited for; matrix products, arithmetic and copies ran while one was open for 2% of the time, Pallas kernels for 0%

commit v1 on v0

v1 whole, which is shorter than its diff:
```python
import functools

import jax
import jax.numpy as jnp
from jax import lax
from jax.experimental import pallas as pl
from jax.experimental.pallas import tpu as pltpu
from jax.sharding import PartitionSpec as P

MESH = pl.DeviceIdType.MESH


def dot(a, b):
    return jnp.dot(a, b, preferred_element_type=jnp.float32)


def split_high_low(values):
    high = values.astype(jnp.bfloat16)
    return high, (values - high.astype(jnp.float32)).astype(jnp.bfloat16)


def kernel(rows, cols, sizes, slot_of, feats, weight, cot, tiles, out, grad_feat, grad_weight,
           slots, dense, flipped, feat_all, pair_send, pair_recv, pair_own, hop_send, hop_recv,
           grad_all, acc, row_send, row_recv, w_term, w_row, w_quarter, w_pair, w_hop, w_all,
           load_sem, feat_s, feat_r, pair_s, pair_r, hop_s, hop_r, gp_s, gp_r, gz_s, gz_r, gf_s, gf_r,
           row_s, row_r, w1_s, w1_r, w2_s, w2_r, w3_s, w3_r, w4_s, w4_r):
    block, tile, row_tiles, col_tiles, slot_total = sizes
    chips = cols // 2
    i = lax.axis_index("row")
    j = lax.axis_index("col")
    q = j // 2
    core = j % 2
    other = 1 - core
    partner = (i, 2 * q + other)

    def row_at(step):
        return lax.rem(i + step, rows)

    def chip_at(step):
        return lax.rem(q + step, chips)

    def send(src, dst, ssem, rsem, device):
        copy = pltpu.make_async_remote_copy(
            src_ref=src, dst_ref=dst, send_sem=ssem, recv_sem=rsem, device_id=device, device_id_type=MESH)
        copy.start()
        return copy

    started = []

    load_tiles = pltpu.make_async_copy(tiles, slots.at[pl.ds(0, slot_total)], load_sem.at[0])
    load_tiles.start()
    own_block = pl.ds(pl.multiple_of(i * block, block), block)
    load_feats = pltpu.make_async_copy(feats, feat_all.at[own_block], load_sem.at[1])
    load_feats.start()

    barrier = pltpu.get_barrier_semaphore()
    peers = [partner]
    for d in range(1, rows):
        peers.append((row_at(d), j))
        peers.append((row_at(d), 2 * q + other))
    for d in range(1, chips):
        peers.append((i, 2 * chip_at(d) + core))
    for peer in peers:
        pl.semaphore_signal(barrier, inc=1, device_id=peer, device_id_type=MESH)
    pl.semaphore_wait(barrier, len(peers))

    feat_copies = []
    for d in range(1, rows):
        feat_copies.append(send(feats, feat_all.at[own_block], feat_s.at[d - 1], feat_r.at[d - 1], (row_at(d), j)))

    slots[slot_total] = jnp.zeros((tile, tile), jnp.bfloat16)
    load_tiles.wait()

    def place(r, carry):
        at = pl.ds(pl.multiple_of(r * tile, tile), tile)
        for c in range(col_tiles):
            dense[at, c * tile:(c + 1) * tile] = slots[slot_of[r * col_tiles + c]]
        return carry

    lax.fori_loop(0, row_tiles, place, 0)

    load_feats.wait()
    for copy in feat_copies:
        copy.wait_recv()
    started += feat_copies

    def partial_of(dest):
        return dot(dense[pl.ds(pl.multiple_of(dest * block, block), block), :], feat_all[...])

    order = list(range(1, chips)) + [0]
    pair_copies = {}
    for d in order:
        pair_send[d] = partial_of(2 * chip_at(d) + other).astype(jnp.bfloat16)
        pair_copies[d] = send(pair_send.at[d], pair_recv.at[d], pair_s.at[d], pair_r.at[d], partner)
    hop_copies = []
    for d in order:
        mine = partial_of(2 * chip_at(d) + core)
        pair_copies[d].wait_recv()
        mine = mine + pair_recv[d].astype(jnp.float32)
        if d:
            hop_send[d - 1] = mine.astype(jnp.bfloat16)
            hop_copies.append(send(hop_send.at[d - 1], hop_recv.at[d - 1], hop_s.at[d - 1], hop_r.at[d - 1],
                                   (i, 2 * chip_at(d) + core)))
        else:
            pair_own[...] = mine
    started += list(pair_copies.values()) + hop_copies

    def turn(r, carry):
        at = pl.ds(pl.multiple_of(r * tile, tile), tile)
        for c in range(col_tiles):
            flipped[c * tile:(c + 1) * tile, at] = dense[at, c * tile:(c + 1) * tile].T
        return carry

    lax.fori_loop(0, row_tiles, turn, 0)

    mixed = pair_own[...]
    for d, copy in enumerate(hop_copies):
        copy.wait_recv()
        mixed = mixed + hop_recv[d].astype(jnp.float32)

    w = weight[...]
    high, low = split_high_low(mixed)
    summed = dot(high, w) + dot(low, w)
    gate = 1.0 / (1.0 + jnp.exp(-summed))
    slope = gate * (1.0 + summed * (1.0 - gate))
    grad = (cot[...].astype(jnp.float32) * slope).astype(jnp.bfloat16)
    grad_all[j] = lax.dot_general(
        grad, w, (((1,), (1,)), ((), ())), preferred_element_type=jnp.float32).astype(jnp.bfloat16)
    gz_copies = []
    for d in order[:-1]:
        gz_copies.append(send(grad_all.at[j], grad_all.at[j], gz_s.at[d - 1], gz_r.at[d - 1],
                              (i, 2 * chip_at(d) + core)))
    gp_copy = send(grad_all.at[j], grad_all.at[j], gp_s.at[0], gp_r.at[0], partner)
    out[...] = (summed * gate).astype(out.dtype)

    mixed_t = mixed.T
    high_t, low_t = split_high_low(mixed_t)
    scale = float(rows * cols * block) ** -0.5
    w_term[...] = (dot(high_t, grad) + dot(low_t, grad)) * scale
    quarter = w_term.shape[0] // rows
    half = quarter // 2

    def quarter_at(index):
        return pl.ds(pl.multiple_of(index * quarter, quarter), quarter)

    w1_copies = []
    for d in range(1, rows):
        w1_copies.append(send(w_term.at[quarter_at(row_at(d))], w_row.at[d - 1], w1_s.at[d - 1], w1_r.at[d - 1],
                              (row_at(d), j)))

    def add_block(source, first):
        term = dot(flipped[:, pl.ds(pl.multiple_of(source * block, block), block)], grad_all[source])
        if first:
            acc[...] = term
        else:
            acc[...] += term

    add_block(j, True)
    gp_copy.wait_recv()
    add_block(2 * q + other, False)

    total = w_term[quarter_at(i)]
    for d, copy in enumerate(w1_copies):
        copy.wait_recv()
        total = total + w_row[d]
    w_quarter[...] = total
    w2_copy = send(w_quarter.at[pl.ds(pl.multiple_of(other * half, half), half)], w_pair, w2_s.at[0], w2_r.at[0],
                   partner)
    started += gz_copies + [gp_copy] + w1_copies + [w2_copy]

    gf_copies = []
    w3_copies = []

    def second_weight_step():
        w2_copy.wait_recv()
        w_hop[q] = w_quarter[pl.ds(pl.multiple_of(core * half, half), half)] + w_pair[...]
        for d in range(1, chips):
            w3_copies.append(send(w_hop.at[q], w_hop.at[q], w3_s.at[d - 1], w3_r.at[d - 1],
                                  (i, 2 * chip_at(d) + core)))

    for d in range(1, chips):
        source = lax.rem(q - d + chips, chips)
        gz_copies[d - 1].wait_recv()
        source_at = 2 * source + core
        gf_copies.append(send(grad_all.at[source_at], grad_all.at[source_at], gf_s.at[d - 1], gf_r.at[d - 1],
                              partner))
        add_block(source_at, False)
        if d == 1:
            second_weight_step()
        gf_copies[d - 1].wait_recv()
        add_block(2 * source + other, False)
    started += gf_copies + w3_copies

    row_copies = []
    for d in range(1, rows):
        at = pl.ds(pl.multiple_of(row_at(d) * block, block), block)
        row_send[d - 1] = acc[at, :].astype(jnp.bfloat16)
        row_copies.append(send(row_send.at[d - 1], row_recv.at[d - 1], row_s.at[d - 1], row_r.at[d - 1],
                               (row_at(d), j)))
    started += row_copies

    for copy in w3_copies:
        copy.wait_recv()
    piece = w_hop[0]
    for k in range(1, chips):
        piece = piece + w_hop[k]
    mine_at = 2 * i + core
    w_all[mine_at] = piece
    w4_copies = []
    for d in range(1, 2 * rows):
        target = (row_at(d // 2), 2 * q + (core if d % 2 == 0 else other))
        w4_copies.append(send(w_all.at[mine_at], w_all.at[mine_at], w4_s.at[d - 1], w4_r.at[d - 1], target))
    started += w4_copies

    final = acc[own_block, :]
    for d, copy in enumerate(row_copies):
        copy.wait_recv()
        final = final + row_recv[d].astype(jnp.float32)
    grad_feat[...] = final.astype(grad_feat.dtype)

    for copy in w4_copies:
        copy.wait_recv()
    grad_weight[...] = w_all[...].reshape(grad_weight.shape)
    for copy in started:
        copy.wait_send()


def local(features, weight, cotangent, tile_values, tile_rows, tile_cols, tile_counts):
    rows = lax.axis_size("row")
    cols = lax.axis_size("col")
    chips = cols // 2
    block, width = features.shape
    hidden = weight.shape[1]
    slot_total, tile = tile_values.shape[2], tile_values.shape[3]
    row_tiles = cols * block // tile
    col_tiles = rows * block // tile
    live = lax.broadcasted_iota(jnp.int32, (slot_total, 1), 0)
    cell = (tile_rows[0, 0] * col_tiles + tile_cols[0, 0])[:, None]
    cells = lax.broadcasted_iota(jnp.int32, (1, row_tiles * col_tiles), 1)
    hit = (cell == cells) & (live < tile_counts[0, 0])
    slot_of = jnp.min(jnp.where(hit, live, slot_total), axis=0)

    half = width // rows // 2
    bf16, f32 = jnp.bfloat16, jnp.float32
    dma = pltpu.SemaphoreType.DMA
    v, any_space = pltpu.VMEM, pl.ANY
    sizes = (block, tile, row_tiles, col_tiles, slot_total)
    scratch = [
        v((slot_total + 1, tile, tile), bf16),
        v((row_tiles * tile, col_tiles * tile), bf16),
        v((col_tiles * tile, row_tiles * tile), bf16),
        v((rows * block, width), bf16),
        v((chips, block, width), bf16),
        v((chips, block, width), bf16),
        v((block, width), f32),
        v((chips - 1, block, width), bf16),
        v((chips - 1, block, width), bf16),
        v((cols, block, width), bf16),
        v((rows * block, width), f32),
        v((rows - 1, block, width), bf16),
        v((rows - 1, block, width), bf16),
        v((width, hidden), f32),
        v((rows - 1, 2 * half, hidden), f32),
        v((2 * half, hidden), f32),
        v((half, hidden), f32),
        v((chips, half, hidden), f32),
        v((2 * rows, half, hidden), f32),
        dma((2,)),
    ]
    for count in (rows - 1, chips, chips - 1, 1, chips - 1, chips - 1, rows - 1, rows - 1, 1, chips - 1,
                  2 * rows - 1):
        scratch += [dma((count,)), dma((count,))]
    vmem = pl.BlockSpec(memory_space=pltpu.VMEM)
    hbm = pl.BlockSpec(memory_space=any_space)
    return pl.pallas_call(
        functools.partial(kernel, rows, cols, sizes),
        out_shape=(
            jax.ShapeDtypeStruct((block, hidden), bf16),
            jax.ShapeDtypeStruct((block, width), bf16),
            jax.ShapeDtypeStruct((width, hidden), f32),
        ),
        in_specs=[pl.BlockSpec(memory_space=pltpu.SMEM), hbm, vmem, vmem, hbm],
        out_specs=(vmem, vmem, vmem),
        scratch_shapes=scratch,
        compiler_params=pltpu.CompilerParams(collective_id=0, has_side_effects=True),
    )(slot_of, features, weight, cotangent, tile_values[0, 0])


def solution(mesh):
    placed = (
        P(("row", "col"), None),
        P(),
        P(("row", "col"), None),
        P("row", "col", None, None, None),
        P("row", "col", None),
        P("row", "col", None),
        P("row", "col"),
    )
    return jax.shard_map(
        local,
        mesh=mesh,
        in_specs=placed,
        out_specs=(P(("row", "col"), None), P(("row", "col"), None), P()),
        check_vma=False,
    )
```

time: 339 us -> 45.3 us (0.13)
  waiting for transfers between devices: 274 us -> 0 us
  Pallas kernels: 0 us -> 37.9 us
  matrix products: 14.5 us -> 0 us
  other arithmetic: 14.7 us -> 1.3 us
  between operations: 14.5 us -> 1.29 us
  blocking collectives: 10.8 us -> 0 us
  local copies, waits for them, and re-layouts: 11.1 us -> 4.61 us
    psum x2 -> x0, waiting for transfers between devices: 198 us -> none  [the longest x1 127 us: local(): grad_weight = lax.psum(weight_term, ('row', 'col')) * node_total ** (-0.5)]
    reduce_scatter x1 -> x0, waiting for transfers between devices: 52.2 us -> none  [local(): lax.psum_scatter(grad_cols, 'row', scatter_dimension=0, tiled=True)]
    pallas_call x0 -> x1, Pallas kernels: none -> 37.9 us  [local(): pl.pallas_call(functools.partial(kernel, rows, cols, sizes), out_shape=(j...]
    all_gather x1 -> x0, waiting for transfers between devices: 22.9 us -> none  [local(): full_cot = lax.all_gather(cotangent, 'col', axis=0, tiled=True)]
    dot_general x5 -> x0, matrix products: 14.5 us -> none  [the longest x2 5.99 us: add_group(): jnp.einsum(pattern, group_values, picked, preferred_element_type=jnp.floa...]
    all_gather x1 -> x0, blocking collectives: 10.8 us -> none  [local(): column_feats = lax.all_gather(features, 'row', axis=0, tiled=True)]
    scatter-add x2 -> x0, other arithmetic: 9.12 us -> none  [add_group(): return running.at[group_rows].add(products)]
    gather x2 -> x0, local copies, waits for them, and re-layouts: 3.55 us -> none  [add_group(): picked = jnp.take(source, group_cols, axis=0)]
  transfers between devices with their start and end apart: 4 -> 0, of which waited for: 4 -> 0; matrix products, arithmetic and copies ran while one was open for 2% -> 0% of each run, Pallas kernels for 0% -> 0%
where the time goes in v1:
time: 45.3 us; the launch traced here: 45.1 us
  Pallas kernels  37.9 us (84%)
  local copies, waits for them, and re-layouts  4.61 us (10%)
  other arithmetic  1.3 us (3%)
  between operations  1.29 us (3%)
    pallas_call x1, Pallas kernels, local(): pl.pallas_call(functools.partial(kernel, rows, cols, sizes), out_shape=(j...  37.9 us
    unnamed x3, local copies, waits for them, and re-layouts  4.61 us

profile of v1, /device:TPU:0, one launch (start us, length us, event | category | flops | bytes accessed | tf_op | source)
XLA Modules:
  0.0 45.1 jit_solution(8539945034400473365)
XLA Ops:
  1.3 0.7 %add_bitcast_fusion = s32[96]{0:T(128)S(1)} fusion(s32[1,1,96]{2,1,0:T(1,128)} %param.12, s32[1,1,96]{2,1,0:T(1,128)} %param.11), kind=kLoop, calls=%fused_computation.4 | loop fusion | flops 192 | bytes 1152 | tf_op jit(solution)/shard_map/add | solution.py:238
  2.0 0.6 %select_reduce_fusion.slot_of = s32[128]{0:T(128)} fusion(s32[96]{0:T(128)S(1)} %add_bitcast_fusion, pred[96]{0:T(512)(128)(4,1)S(1)} %iota_compare_fusion.1), kind=kLoop, calls=%fused_computation | loop fusion | flops 49024 | bytes 992 | tf_op jit(solution)/shard_map/reduce_min | solution.py:241
  2.6 37.9 %shard_map.94 = (bf16[256,256]{1,0:T(8,128)(2,1)}, bf16[256,128]{1,0:T(8,128)(2,1)}, f32[128,256]{1,0:T(8,128)}) custom-call(s32[128]{0:T(128)} %select_reduce_fusion.slot_of, bf16[256,128]{1,0:T(8,128)(2,1)} %feats.1, bf16[128,256]{1,0:T(8,128)(2,1)} %weight.1, bf16[256,256]{1,0:T(8,128)(2,1)} %cot.1, bf16[96,128,128]{2,1,0:T(8,128)(2,1)} %bitcast.5), custom_call_target="tpu_custom_call" | custom-call | tf_op jit(solution)/shard_map/pallas_call | solution.py:275
  40.5 1.6 %copy.14 = bf16[256,256]{1,0:T(8,128)(2,1)} copy(bf16[256,256]{1,0:T(8,128)(2,1)} %get-tuple-element.6) | data formatting | bytes 262144
  42.1 1.5 %copy.15 = bf16[256,128]{1,0:T(8,128)(2,1)} copy(bf16[256,128]{1,0:T(8,128)(2,1)} %get-tuple-element.7) | data formatting | bytes 131072
  43.5 1.6 %copy.16 = f32[128,256]{1,0:T(8,128)} copy(f32[128,256]{1,0:T(8,128)} %get-tuple-element.8) | data formatting | bytes 262144
  (1 shorter events, 0.0 us)

commit v2 on v1

--- a/solution.py
+++ b/solution.py
@@ -19,8 +19,14 @@
     return high, (values - high.astype(jnp.float32)).astype(jnp.bfloat16)
 
 
-def kernel(rows, cols, sizes, slot_of, feats, weight, cot, tiles, out, grad_feat, grad_weight,
-           slots, dense, flipped, feat_all, pair_send, pair_recv, pair_own, hop_send, hop_recv,
+def finish(*refs):
+    count = len(refs) // 2
+    for source, result in zip(refs[:count], refs[count:]):
+        result[...] = source[...]
+
+
+def kernel(rows, cols, sizes, live_count, tile_row, tile_col, feats, weight, cot, tiles, out, grad_feat, grad_weight,
+           keys, table, slot_of, summing, slots, dense, flipped, feat_all, pair_send, pair_recv, pair_own, hop_send, hop_recv,
            grad_all, acc, row_send, row_recv, w_term, w_row, w_quarter, w_pair, w_hop, w_all,
            load_sem, feat_s, feat_r, pair_s, pair_r, hop_s, hop_r, gp_s, gp_r, gz_s, gz_r, gf_s, gf_r,
            row_s, row_r, w1_s, w1_r, w2_s, w2_r, w3_s, w3_r, w4_s, w4_r):
@@ -37,7 +43,14 @@
         return lax.rem(i + step, rows)
 
     def chip_at(step):
-        return lax.rem(q + step, chips)
+        if chips & (chips - 1):
+            return lax.rem(chips + step - q, chips)
+        paired, bit = q, 1
+        while bit <= step:
+            if step & bit:
+                paired = paired + bit - 2 * bit * ((q // bit) % 2)
+            bit *= 2
+        return paired
 
     def send(src, dst, ssem, rsem, device):
         copy = pltpu.make_async_remote_copy(
@@ -62,48 +75,82 @@
         peers.append((i, 2 * chip_at(d) + core))
     for peer in peers:
         pl.semaphore_signal(barrier, inc=1, device_id=peer, device_id_type=MESH)
+
+    cell_total = row_tiles * col_tiles
+    lanes = lax.broadcasted_iota(jnp.int32, (1, slot_total), 1)
+    keys[...] = jnp.full(keys.shape, -1, jnp.int32)
+    keys[:, :slot_total] = jnp.where(lanes < live_count[0, 0], tile_row[...] * col_tiles + tile_col[...], -1)
+    padded = keys.shape[1]
+    key_columns = jnp.broadcast_to(keys[...], (128, padded)).T
+    slot_ids = lax.broadcasted_iota(jnp.int32, (padded, 128), 0) - slot_total
+    cell_ids = lax.broadcasted_iota(jnp.int32, (padded, 128), 1)
+    for first in range(0, cell_total, 128):
+        found = jnp.where(key_columns == cell_ids + first, slot_ids, 0)
+        table[:, first:first + 128] = jnp.sum(found, axis=0, keepdims=True) + slot_total
+    load_table = pltpu.make_async_copy(table, slot_of, load_sem.at[2])
+    load_table.start()
+    slots[slot_total] = jnp.zeros((tile, tile), jnp.bfloat16)
     pl.semaphore_wait(barrier, len(peers))
 
     feat_copies = []
     for d in range(1, rows):
         feat_copies.append(send(feats, feat_all.at[own_block], feat_s.at[d - 1], feat_r.at[d - 1], (row_at(d), j)))
 
-    slots[slot_total] = jnp.zeros((tile, tile), jnp.bfloat16)
+    load_table.wait()
     load_tiles.wait()
 
     def place(r, carry):
         at = pl.ds(pl.multiple_of(r * tile, tile), tile)
         for c in range(col_tiles):
-            dense[at, c * tile:(c + 1) * tile] = slots[slot_of[r * col_tiles + c]]
+            dense[at, c * tile:(c + 1) * tile] = slots[slot_of[0, r * col_tiles + c]]
         return carry
 
     lax.fori_loop(0, row_tiles, place, 0)
 
+    def product_at(at, source):
+        source_at = pl.ds(pl.multiple_of(source * block, block), block)
+        return dot(dense[at, source_at], feat_all[source_at, :])
+
     load_feats.wait()
-    for copy in feat_copies:
-        copy.wait_recv()
+    for d in range(rows - 1):
+        if d:
+            feat_copies[d - 1].wait_recv()
+        source = lax.rem(i - d + rows, rows)
+
+        def add_source(dest, carry):
+            at = pl.ds(pl.multiple_of(dest * block, block), block)
+            if d:
+                summing[at, :] += product_at(at, source)
+            else:
+                summing[at, :] = product_at(at, source)
+            return carry
+
+        lax.fori_loop(0, cols, add_source, 0)
+    feat_copies[rows - 2].wait_recv()
+    last = lax.rem(i + 1, rows)
+
+    def partial_of(dest):
+        at = pl.ds(pl.multiple_of(dest * block, block), block)
+        return summing[at, :] + product_at(at, last)
+
     started += feat_copies
-
-    def partial_of(dest):
-        return dot(dense[pl.ds(pl.multiple_of(dest * block, block), block), :], feat_all[...])
-
-    order = list(range(1, chips)) + [0]
+    order = list(range(chips - 1, -1, -1))
     pair_copies = {}
     for d in order:
         pair_send[d] = partial_of(2 * chip_at(d) + other).astype(jnp.bfloat16)
         pair_copies[d] = send(pair_send.at[d], pair_recv.at[d], pair_s.at[d], pair_r.at[d], partner)
-    hop_copies = []
+    hop_copies = {}
     for d in order:
         mine = partial_of(2 * chip_at(d) + core)
         pair_copies[d].wait_recv()
         mine = mine + pair_recv[d].astype(jnp.float32)
         if d:
             hop_send[d - 1] = mine.astype(jnp.bfloat16)
-            hop_copies.append(send(hop_send.at[d - 1], hop_recv.at[d - 1], hop_s.at[d - 1], hop_r.at[d - 1],
-                                   (i, 2 * chip_at(d) + core)))
+            hop_copies[d] = send(hop_send.at[d - 1], hop_recv.at[d - 1], hop_s.at[d - 1], hop_r.at[d - 1],
+                                 (i, 2 * chip_at(d) + core))
         else:
             pair_own[...] = mine
-    started += list(pair_copies.values()) + hop_copies
+    started += list(pair_copies.values()) + list(hop_copies.values())
 
     def turn(r, carry):
         at = pl.ds(pl.multiple_of(r * tile, tile), tile)
@@ -114,9 +161,9 @@
     lax.fori_loop(0, row_tiles, turn, 0)
 
     mixed = pair_own[...]
-    for d, copy in enumerate(hop_copies):
-        copy.wait_recv()
-        mixed = mixed + hop_recv[d].astype(jnp.float32)
+    for d in range(1, chips):
+        hop_copies[d].wait_recv()
+        mixed = mixed + hop_recv[d - 1].astype(jnp.float32)
 
     w = weight[...]
     high, low = split_high_low(mixed)
@@ -126,10 +173,10 @@
     grad = (cot[...].astype(jnp.float32) * slope).astype(jnp.bfloat16)
     grad_all[j] = lax.dot_general(
         grad, w, (((1,), (1,)), ((), ())), preferred_element_type=jnp.float32).astype(jnp.bfloat16)
-    gz_copies = []
+    gz_copies = {}
     for d in order[:-1]:
-        gz_copies.append(send(grad_all.at[j], grad_all.at[j], gz_s.at[d - 1], gz_r.at[d - 1],
-                              (i, 2 * chip_at(d) + core)))
+        gz_copies[d] = send(grad_all.at[j], grad_all.at[j], gz_s.at[d - 1], gz_r.at[d - 1],
+                            (i, 2 * chip_at(d) + core))
     gp_copy = send(grad_all.at[j], grad_all.at[j], gp_s.at[0], gp_r.at[0], partner)
     out[...] = (summed * gate).astype(out.dtype)
 
@@ -166,7 +213,7 @@
     w_quarter[...] = total
     w2_copy = send(w_quarter.at[pl.ds(pl.multiple_of(other * half, half), half)], w_pair, w2_s.at[0], w2_r.at[0],
                    partner)
-    started += gz_copies + [gp_copy] + w1_copies + [w2_copy]
+    started += list(gz_copies.values()) + [gp_copy] + w1_copies + [w2_copy]
 
     gf_copies = []
     w3_copies = []
@@ -179,8 +226,8 @@
                                   (i, 2 * chip_at(d) + core)))
 
     for d in range(1, chips):
-        source = lax.rem(q - d + chips, chips)
-        gz_copies[d - 1].wait_recv()
+        source = chip_at(d)
+        gz_copies[d].wait_recv()
         source_at = 2 * source + core
         gf_copies.append(send(grad_all.at[source_at], grad_all.at[source_at], gf_s.at[d - 1], gf_r.at[d - 1],
                               partner))
@@ -234,18 +281,17 @@
     slot_total, tile = tile_values.shape[2], tile_values.shape[3]
     row_tiles = cols * block // tile
     col_tiles = rows * block // tile
-    live = lax.broadcasted_iota(jnp.int32, (slot_total, 1), 0)
-    cell = (tile_rows[0, 0] * col_tiles + tile_cols[0, 0])[:, None]
-    cells = lax.broadcasted_iota(jnp.int32, (1, row_tiles * col_tiles), 1)
-    hit = (cell == cells) & (live < tile_counts[0, 0])
-    slot_of = jnp.min(jnp.where(hit, live, slot_total), axis=0)
-
+    cell_total = row_tiles * col_tiles
     half = width // rows // 2
     bf16, f32 = jnp.bfloat16, jnp.float32
     dma = pltpu.SemaphoreType.DMA
     v, any_space = pltpu.VMEM, pl.ANY
     sizes = (block, tile, row_tiles, col_tiles, slot_total)
     scratch = [
+        v((1, pl.cdiv(slot_total, 128) * 128), jnp.int32),
+        v((1, cell_total), jnp.int32),
+        pltpu.SMEM((1, cell_total), jnp.int32),
+        v((row_tiles * tile, width), f32),
         v((slot_total + 1, tile, tile), bf16),
         v((row_tiles * tile, col_tiles * tile), bf16),
         v((col_tiles * tile, row_tiles * tile), bf16),
@@ -265,25 +311,32 @@
         v((half, hidden), f32),
         v((chips, half, hidden), f32),
         v((2 * rows, half, hidden), f32),
-        dma((2,)),
+        dma((3,)),
     ]
     for count in (rows - 1, chips, chips - 1, 1, chips - 1, chips - 1, rows - 1, rows - 1, 1, chips - 1,
                   2 * rows - 1):
         scratch += [dma((count,)), dma((count,))]
     vmem = pl.BlockSpec(memory_space=pltpu.VMEM)
     hbm = pl.BlockSpec(memory_space=any_space)
-    return pl.pallas_call(
+    results = (
+        jax.ShapeDtypeStruct((block, hidden), bf16),
+        jax.ShapeDtypeStruct((block, width), bf16),
+        jax.ShapeDtypeStruct((width, hidden), f32),
+    )
+    values = pl.pallas_call(
         functools.partial(kernel, rows, cols, sizes),
-        out_shape=(
-            jax.ShapeDtypeStruct((block, hidden), bf16),
-            jax.ShapeDtypeStruct((block, width), bf16),
-            jax.ShapeDtypeStruct((width, hidden), f32),
-        ),
-        in_specs=[pl.BlockSpec(memory_space=pltpu.SMEM), hbm, vmem, vmem, hbm],
+        out_shape=results,
+        in_specs=[pl.BlockSpec(memory_space=pltpu.SMEM), vmem, vmem, hbm, vmem, vmem, hbm],
         out_specs=(vmem, vmem, vmem),
         scratch_shapes=scratch,
         compiler_params=pltpu.CompilerParams(collective_id=0, has_side_effects=True),
-    )(slot_of, features, weight, cotangent, tile_values[0, 0])
+    )(tile_counts, tile_rows[0], tile_cols[0], features, weight, cotangent, tile_values[0, 0])
+    return pl.pallas_call(
+        finish,
+        out_shape=results,
+        in_specs=[vmem] * 3,
+        out_specs=(vmem, vmem, vmem),
+    )(*values)
 
 
 def solution(mesh):

time: 45.3 us -> 42.2 us (0.932)
  local copies, waits for them, and re-layouts: 4.61 us -> 0 us
  Pallas kernels: 37.9 us -> 40.8 us
  other arithmetic: 1.3 us -> 0 us
    unnamed x3 -> x0, local copies, waits for them, and re-layouts: 4.61 us -> none
    pallas_call x1 -> x2, Pallas kernels: 37.9 us -> 40.8 us  [the longest x1 39 us: local(): pl.pallas_call(functools.partial(kernel, rows, cols, sizes), out_shape=re...]
    add x1 -> x0, other arithmetic: 0.68 us -> none  [local(): cell = (tile_rows[0, 0] * col_tiles + tile_cols[0, 0])[:, None]]
    reduce_min x1 -> x0, other arithmetic: 0.62 us -> none  [local(): slot_of = jnp.min(jnp.where(hit, live, slot_total), axis=0)]
where the time goes in v2:
time: 42.2 us; the launch traced here: 42 us
  Pallas kernels  40.8 us (97%)
  between operations  1.29 us (3%)
    pallas_call x1, Pallas kernels, local(): pl.pallas_call(functools.partial(kernel, rows, cols, sizes), out_shape=re...  39 us
    pallas_call x1, Pallas kernels, local(): pl.pallas_call(finish, out_shape=results, in_specs=[vmem] * 3, out_specs=...  1.73 us

profile of v2, /device:TPU:0, one launch (start us, length us, event | category | flops | bytes accessed | tf_op | source)
XLA Modules:
  0.0 42.0 jit_solution(12754825871713404532)
XLA Ops:
  1.3 39.0 %shard_map.94 = (bf16[256,256]{1,0:T(8,128)(2,1)}, bf16[256,128]{1,0:T(8,128)(2,1)}, f32[128,256]{1,0:T(8,128)}) custom-call(s32[1,1]{1,0:T(1,128)S(6)} %copy.10.live_count, s32[1,96]{1,0:T(1,128)} %bitcast.4, s32[1,96]{1,0:T(1,128)} %bitcast.5, bf16[256,128]{1,0:T(8,128)(2,1)} %feats.1, bf16[128,256]{1,0:T(8,128)(2,1)} %weight.1, bf16[256,256]{1,0:T(8,128)(2,1)} %cot.1, ...), custom_call_target="tpu_custom_call" | custom-call | tf_op jit(solution)/shard_map/pallas_call | solution.py:326
  40.3 1.7 %shard_map.95 = (bf16[256,256]{1,0:T(8,128)(2,1)}, bf16[256,128]{1,0:T(8,128)(2,1)}, f32[128,256]{1,0:T(8,128)}) custom-call(bf16[256,256]{1,0:T(8,128)(2,1)} %get-tuple-element.6.refs_0_, bf16[256,128]{1,0:T(8,128)(2,1)} %get-tuple-element.7.refs_1_, f32[128,256]{1,0:T(8,128)} %get-tuple-element.8.refs_2_), custom_call_target="tpu_custom_call" | custom-call | tf_op jit(solution)/shard_map/pallas_call | solution.py:334
